TPU v7x, 128 devices: a whole 4x4x4 slice. The times are simulated.
128 devices in a mesh: sect: 2 (over y_hi), seq: 64 (over z, x, y_lo, core).
Axes of the slice: x: 4, y: 4 (y_hi: 2, y_lo: 2; y = y_hi * 2 + y_lo), z: 4, core: 2. Of those that a mesh axis runs over, the one named last changes fastest.
Arguments:
- queries: bfloat16 [4096, 8192], P('seq'), may hold values from -160 to 160
- key_tokens: bfloat16 [4096, 8192], P('seq'), may hold values from -6 to 6
- value_tokens: bfloat16 [4096, 8192], P('seq'), may hold values from -17 to 17
- latent: bfloat16 [256, 2560], P('seq'), may hold values from -6 to 6
- tile_rows: int32 [64], replicated, may hold values from 1 to 4, 128 in all
- conv_in_weight: bfloat16 [3, 3, 3, 16, 384], replicated, may hold values from -0.3125 to 0.3125
- conv_in_bias: float32 [384], replicated, may hold values from -3 to 3
- norm_gain: float32 [384], replicated, may hold values from 0.5 to 2
- conv_mid_weight: bfloat16 [3, 3, 3, 384, 384], replicated, may hold values from -0.0625 to 0.0625
- conv_mid_bias: float32 [384], replicated, may hold values from -3 to 3
Outputs:
- attended: bfloat16 [4096, 8192], P('seq', 'sect')
- frames: bfloat16 [2, 512, 80, 384], P(None, 'seq', 'sect')
Inputs may be any that keep to these rules, and one draw needn't show every extreme that they name: `tile_rows`: the tiles cover the 128 token rows in order; some tile has exactly 4 rows.
All inputs are finite; a program needn't handle non-finite values.
Results may differ from a plain program's by a relative error of at most 0.012.
Values may be sent and summed in bfloat16 or wider, within the bound.
A program may use at most 128 MiB of HBM per device.

v0:
```python
import functools
import math

import jax
import jax.numpy as jnp
from jax import lax
from jax.experimental import pallas as pl
from jax.experimental.pallas import tpu as pltpu
from jax.sharding import PartitionSpec as P

BF = jnp.bfloat16
F32 = jnp.float32
MESH = pl.DeviceIdType.MESH

DH = 128
ROWS = 64
PEERS = 32
KEYS = 4096
OWN = 2048
BQ = 256
BK = 1024
NB = OWN // BQ
GROUP = 8
GROUPS = PEERS // GROUP
CH = 384
LATW = 1536
LF = 2
OUT_ROWS = 8
COLS = 40
NT = (((1,), (1,)), ((), ()))
EXP2_SCALE = math.log2(math.e) / math.sqrt(DH)


def body(
    tile_rows,
    q,
    k,
    v,
    latent,
    w_in,
    b_in,
    gain,
    w_mid,
    b_mid,
    attended,
    frames,
    kbuf,
    vbuf,
    qbuf,
    obuf,
    vt,
    sbuf,
    mbuf,
    latbuf,
    picked,
    patches,
    win,
    ybuf,
    ring,
    hidden,
    activated,
    wm,
    fbuf,
    s_k,
    s_v,
    s_q,
    s_o,
    s_l,
    r_k,
    r_v,
    r_q,
    r_o,
    r_l,
    fs_k,
    fs_v,
    fs_l,
    fr_k,
    fr_v,
    fr_l,
    w_sem,
    win_sem,
    out_sem,
):
    sect = lax.axis_index("sect")
    me = lax.axis_index("seq")
    core = me % 2
    chip = me // 2
    y = chip % 2
    x = (chip // 2) % 4
    z = chip // 8

    def peer(t, sign=1):
        dz, dx, dy = t // 8, (t // 2) % 4, t % 2
        return (((z + sign * dz + 4) % 4) * 4 + (x + sign * dx + 4) % 4) * 2 + (y + dy) % 2

    def device(other_chip, other_core):
        return (sect, other_chip * 2 + other_core)

    sibling = device(chip, 1 - core)

    def remote(src, dst, send_sem, recv_sem, target):
        return pltpu.make_async_remote_copy(
            src, dst, send_sem, recv_sem, device_id=target, device_id_type=MESH
        )

    barrier = pltpu.get_barrier_semaphore()
    pl.semaphore_signal(barrier, inc=1, device_id=sibling, device_id_type=MESH)

    @pl.loop(1, PEERS)
    def _(t):
        pl.semaphore_signal(barrier, inc=1, device_id=device(peer(t), core), device_id_type=MESH)

    pl.semaphore_wait(barrier, PEERS)

    def head_columns(other_chip):
        return pl.ds(pl.multiple_of((PEERS * sect + other_chip) * DH, DH), DH)

    def slot(t):
        return pl.ds(pl.multiple_of(t * ROWS, ROWS), ROWS)

    def core_slot(t):
        return pl.ds(pl.multiple_of(core * OWN + t * ROWS, ROWS), ROWS)

    def lat_needed(holder, tile_chip):
        low = jnp.maximum(2 * tile_chip, 8 * tile_chip - 128) - 1
        high = jnp.minimum(8 * tile_chip + 4, 65 + 2 * tile_chip) + 4
        first = 8 * (holder % 16)
        return (first + 7 >= low) & (first <= high)

    lat_cols = pl.ds(pl.multiple_of(1024 * sect, 128), LATW)

    @pl.when(lat_needed(chip, chip))
    def _():
        pltpu.make_async_copy(latent.at[:, lat_cols], latbuf.at[core * PEERS], r_l.at[0]).start()

    @pl.loop(1, PEERS)
    def _(t):
        other = peer(t)

        @pl.when(lat_needed(chip, other))
        def _():
            remote(
                latent.at[:, lat_cols],
                latbuf.at[core * PEERS + t],
                s_l.at[t],
                r_l.at[t],
                device(other, core),
            ).start()

    mine = head_columns(chip)
    pltpu.make_async_copy(k.at[:, mine], kbuf.at[core_slot(0)], r_k.at[0]).start()
    pltpu.make_async_copy(v.at[:, mine], vbuf.at[core_slot(0)], r_v.at[0]).start()

    @pl.loop(1, PEERS)
    def _(t):
        other = peer(t)
        target = device(other, core)
        cols = head_columns(other)
        group = t // GROUP
        remote(k.at[:, cols], kbuf.at[core_slot(t)], s_k, r_k.at[group], target).start()
        remote(v.at[:, cols], vbuf.at[core_slot(t)], s_v, r_v.at[group], target).start()

    pltpu.make_async_copy(q.at[:, mine], qbuf.at[slot(0)], r_q.at[0]).start()

    @pl.loop(1, PEERS)
    def _(t):
        other = peer(t)
        remote(
            q.at[:, head_columns(other)], qbuf.at[slot(t)], s_q, r_q.at[t // 4], device(other, core)
        ).start()

    for a in range(1, 3):
        pltpu.make_async_copy(w_mid.at[a], wm.at[a - 1], w_sem).start()
    win[...] = jnp.zeros_like(win)
    for a in range(1, 3):
        for out_p in range(2):
            for out_q in range(2):
                for tap_b in range(3):
                    for tap_e in range(3):
                        cell_r, cell_c = out_p + tap_b, out_q + tap_e
                        far_row, p = (0, cell_r - 1) if cell_r in (1, 2) else (1, 0 if cell_r else 1)
                        far_col, qq = (0, cell_c - 1) if cell_c in (1, 2) else (1, 0 if cell_c else 1)
                        row = (2 - a) * 256 + far_row * 128 + far_col * 64 + p * 32 + qq * 16
                        col = (out_p * 2 + out_q) * CH
                        pltpu.make_async_copy(
                            w_in.at[a, tap_b, tap_e],
                            win.at[row : row + 16, col : col + CH],
                            win_sem,
                        ).start()
    vt[DH:, :] = jnp.ones((16, KEYS), BF)
    ring[...] = jnp.zeros_like(ring)
    picked[...] = jnp.zeros_like(picked)

    def count(d, total):
        return total + jnp.where(d < me, tile_rows[d], 0)

    first_row = lax.fori_loop(0, 64, count, jnp.int32(0))
    filled = tile_rows[me]

    @pl.loop(0, PEERS)
    def _(t):
        @pl.when(lat_needed(peer(t, -1), chip))
        def _():
            here = latbuf.at[core * PEERS + t]
            remote(here, here, fs_l.at[t], r_l.at[t], sibling).wait_recv()
            remote(here, here, fs_l.at[t], fr_l.at[t], sibling).start()

    @pl.loop(0, PEERS)
    def _(t):
        @pl.when(lat_needed(peer(t, -1), chip))
        def _():
            there = latbuf.at[(1 - core) * PEERS + t]
            remote(there, there, fs_l.at[t], fr_l.at[t], sibling).wait_recv()

    def group_rows(which, g):
        return pl.ds(which * OWN + g * GROUP * ROWS, GROUP * ROWS)

    def hand_on(g):
        rows = group_rows(core, g)
        remote(kbuf.at[rows], kbuf.at[rows], fs_k, r_k.at[g], sibling).wait_recv()
        remote(kbuf.at[rows], kbuf.at[rows], fs_k, fr_k.at[g], sibling).start()
        remote(vbuf.at[rows], vbuf.at[rows], fs_v, r_v.at[g], sibling).wait_recv()
        remote(vbuf.at[rows], vbuf.at[rows], fs_v, fr_v.at[g], sibling).start()

    sub_iota = lax.broadcasted_iota(jnp.int32, (4, LATW), 0)
    for f in range(LF):
        for r in range(6):
            g = first_row - 1 + r
            inside = (g >= 0) & (g < 128)
            safe = jnp.clip(g, 0, 127)
            holder = f * 32 + safe // 4
            other = holder // 2
            dz = (z - other // 8 + 4) % 4
            dx = (x - (other // 2) % 4 + 4) % 4
            dy = (y - other % 2 + 2) % 2
            rows4 = latbuf[(holder % 2) * PEERS + dz * 8 + dx * 2 + dy].astype(F32)
            wanted = jnp.where(inside, safe % 4, -1)
            row = jnp.sum(jnp.where(sub_iota == wanted, rows4, 0.0), axis=0, keepdims=True)
            picked[f * 8 + r : f * 8 + r + 1, :] = row

    lane = lax.broadcasted_iota(jnp.int32, (16, 128), 1)
    far = lane >= 64
    p_bit = (lane // 32) % 2
    q_bit = (lane // 16) % 2
    blank = jnp.zeros((16, 128), F32)
    pairs = [picked[:, j * 128 : (j + 1) * 128] for j in range(12)]
    swapped = [pltpu.roll(pair, 64, 1) for pair in pairs]
    for j in range(12):
        before = pairs[j - 1] if j > 0 else blank
        after = swapped[j + 1] if j < 11 else blank
        even = jnp.where(far & (q_bit == 1), before, pairs[j])
        odd = jnp.where(far & (q_bit == 0), after, swapped[j])
        for parity, token in enumerate((even, odd)):
            below = pltpu.roll(token, 15, 0)
            above = pltpu.roll(token, 1, 0)
            rim = jnp.where(p_bit == 0, below, above)
            at = (2 * j + parity) * 16
            patches[at : at + 16, 0:128] = token.astype(BF)
            patches[at : at + 16, 128:256] = rim.astype(BF)
            zero8 = jnp.zeros((8, 128), F32)
            patches[at : at + 16, 256:384] = jnp.concatenate([zero8, token[0:8]], axis=0).astype(BF)
            patches[at : at + 16, 384:512] = jnp.concatenate([zero8, rim[0:8]], axis=0).astype(BF)

    pltpu.make_async_copy(win.at[0:288], win.at[0:288], win_sem).wait()
    for n in range(4):
        conv = jnp.dot(patches[...], win[:, n * CH : (n + 1) * CH], preferred_element_type=F32)
        for part in range(3):
            ybuf[n * 3 + part] = conv[:, part * 128 : (part + 1) * 128]

    hand_on(0)

    bias_in = b_in[...].reshape(1, CH)
    gain_row = gain[...].reshape(1, CH)
    bias_mid = b_mid[...].reshape(1, CH)

    @pl.loop(0, LF)
    def _(f):
        for hr in range(10):
            r, p = (hr + 1) // 2, (hr + 1) % 2
            grid_row = 2 * first_row + hr - 1
            row_valid = (grid_row >= 0) & (grid_row < 256)
            for qq in range(2):
                n = 2 * p + qq
                conv = jnp.concatenate(
                    [ybuf[n * 3 + part, pl.ds(f * 8 + r, 24, stride=16), :] for part in range(3)],
                    axis=1,
                )
                wide = (conv + bias_in).astype(BF).astype(F32)
                mean = jnp.sum(wide * wide, axis=1, keepdims=True) * (1.0 / CH)
                scaled = wide * lax.rsqrt(mean + 1e-6) * gain_row
                act = scaled / (1.0 + jnp.exp(-scaled))
                act = jnp.where(row_valid, act, 0.0)
                for part in range(3):
                    lanes = slice(part * 128, (part + 1) * 128)
                    for e in range(3):
                        ring[e, part, pl.ds(9 - e + qq, 24, stride=2), :] = act[:, lanes]
                    hidden[f, hr, part, pl.ds(qq, 24, stride=2), :] = wide[:, lanes]
            for e in range(3):
                for part in range(3):
                    cut = ring[e, part, pl.ds(pl.multiple_of(8 * sect + 8, 8), COLS), :]
                    at = e * CH + part * 128
                    activated[f, hr * COLS : (hr + 1) * COLS, at : at + 128] = cut.astype(BF)

    hand_on(1)

    pltpu.make_async_copy(wm, wm, w_sem).wait()
    for f in range(LF):
        total = None
        for a in range(3):
            source = f + a - 2
            if source < 0:
                continue
            for b in range(3):
                rows = activated[source, b * COLS : (b + OUT_ROWS) * COLS, :]
                weights = wm[a - 1, b * 3 * CH : (b + 1) * 3 * CH, :]
                part = jnp.dot(rows, weights, preferred_element_type=F32)
                total = part if total is None else total + part
        for ro in range(OUT_ROWS):
            cut = pl.ds(pl.multiple_of(8 * sect, 8), COLS)
            centre = jnp.concatenate(
                [hidden[f, ro + 1, part, cut, :] for part in range(3)], axis=1
            )
            value = total[ro * COLS : (ro + 1) * COLS, :] + bias_mid + centre
            fbuf[f, ro] = jnp.where(ro < 2 * filled, value, 0.0).astype(BF)
        hand_on(2 + f)
    pltpu.make_async_copy(fbuf, frames, out_sem).start()

    for which in range(2):
        for g in range(GROUPS):
            rows = slice(which * OWN + g * GROUP * ROWS, which * OWN + (g + 1) * GROUP * ROWS)

            @pl.when(core != which)
            def _():
                remote(kbuf.at[rows], kbuf.at[rows], fs_k, fr_k.at[g], sibling).wait_recv()
                remote(vbuf.at[rows], vbuf.at[rows], fs_v, fr_v.at[g], sibling).wait_recv()

            vt[0:DH, rows] = vbuf[rows, :].T

    def block(j):
        return pl.ds(pl.multiple_of(j * BQ, BQ), BQ)

    def await_queries(j):
        rows = qbuf.at[block(j)]
        remote(rows, rows, s_q, r_q.at[j], sibling).wait_recv()

    def score_chunk(q_block, which, c, best):
        part = lax.dot_general(
            kbuf[c * BK : (c + 1) * BK, :], q_block, NT, preferred_element_type=F32
        )
        sbuf[which, c * BK : (c + 1) * BK, :] = part
        return jnp.maximum(best, jnp.max(part.reshape(BK // 8, 8, BQ), axis=0))

    def keep_best(best, which):
        top = jnp.max(best, axis=0, keepdims=True) * EXP2_SCALE
        mbuf[which] = jnp.broadcast_to(top, (8, BQ))

    def step(j, with_next):
        which = j % 2
        total = jnp.zeros((DH + 8, BQ), F32)
        if with_next:
            await_queries(j + 1)
            q_next = qbuf[block(j + 1), :]
            best = jnp.full((8, BQ), -jnp.inf, F32)
        top = mbuf[which, 0:1, :]
        for c in range(KEYS // BK):
            if with_next:
                best = score_chunk(q_next, 1 - which, c, best)
            scores = sbuf[which, c * BK : (c + 1) * BK, :]
            weights = jnp.exp2(scores * EXP2_SCALE - top).astype(BF)
            total = total + jnp.dot(
                vt[0 : DH + 8, c * BK : (c + 1) * BK], weights, preferred_element_type=F32
            )
        if with_next:
            keep_best(best, 1 - which)
        obuf[block(j), :] = (total[0:DH, :] / total[DH : DH + 1, :]).T.astype(BF)
        for u in range(BQ // ROWS):
            t = j * (BQ // ROWS) + u

            def send():
                remote(
                    obuf.at[slot(t)], attended.at[:, out_cols], s_o, r_o, device(peer(t, -1), core)
                ).start()

            if u > 0:
                send()
            else:
                pl.when(t > 0)(send)

                @pl.when(t == 0)
                def _():
                    pltpu.make_async_copy(obuf.at[slot(0)], attended.at[:, out_cols], r_o).start()

    out_cols = pl.ds(pl.multiple_of(chip * DH, DH), DH)
    await_queries(0)
    best = jnp.full((8, BQ), -jnp.inf, F32)
    q_first = qbuf[0:BQ, :]
    for c in range(KEYS // BK):
        best = score_chunk(q_first, 0, c, best)
    keep_best(best, 0)

    @pl.loop(0, NB - 1)
    def _(j):
        step(j, True)

    step(jnp.int32(NB - 1), False)

    own = pl.ds(core * OWN, OWN)
    most = kbuf.at[0 : (PEERS - 1) * ROWS]
    remote(most, most, s_k, r_o, sibling).wait_send()
    remote(most, most, s_v, r_o, sibling).wait_send()
    remote(most, most, s_q, r_o, sibling).wait_send()
    remote(kbuf.at[own], kbuf.at[own], fs_k, r_o, sibling).wait_send()
    remote(kbuf.at[own], kbuf.at[own], fs_v, r_o, sibling).wait_send()

    @pl.loop(0, PEERS)
    def _(t):
        @pl.when(lat_needed(peer(t, -1), chip))
        def _():
            here = latbuf.at[core * PEERS + t]
            remote(here, here, fs_l.at[t], r_o, sibling).wait_send()

        @pl.when((t > 0) & lat_needed(chip, peer(t)))
        def _():
            here = latbuf.at[core * PEERS + t]
            remote(here, here, s_l.at[t], r_o, sibling).wait_send()

    pltpu.make_async_copy(fbuf, frames, out_sem).wait()
    remote(most, most, s_o, r_o, sibling).wait_send()
    remote(attended, attended, s_o, r_o, sibling).wait_recv()


def on_device(
    queries,
    key_tokens,
    value_tokens,
    latent,
    tile_rows,
    conv_in_weight,
    conv_in_bias,
    norm_gain,
    conv_mid_weight,
    conv_mid_bias,
):
    dma = pltpu.SemaphoreType.DMA
    anywhere = pl.BlockSpec(memory_space=pl.ANY)
    vmem = pl.BlockSpec(memory_space=pltpu.VMEM)
    smem = pl.BlockSpec(memory_space=pltpu.SMEM)
    return pl.pallas_call(
        body,
        out_shape=(
            jax.ShapeDtypeStruct((ROWS, PEERS * DH), BF),
            jax.ShapeDtypeStruct((LF, OUT_ROWS, COLS, CH), BF),
        ),
        in_specs=[smem] + [anywhere] * 5 + [vmem, vmem, anywhere, vmem],
        out_specs=(anywhere, anywhere),
        scratch_shapes=[
            pltpu.VMEM((KEYS, DH), BF),
            pltpu.VMEM((KEYS, DH), BF),
            pltpu.VMEM((OWN, DH), BF),
            pltpu.VMEM((OWN, DH), BF),
            pltpu.VMEM((DH + 16, KEYS), BF),
            pltpu.VMEM((2, KEYS, BQ), F32),
            pltpu.VMEM((2, 8, BQ), F32),
            pltpu.VMEM((2 * PEERS, 4, LATW), BF),
            pltpu.VMEM((16, LATW), F32),
            pltpu.VMEM((384, 512), BF),
            pltpu.VMEM((512, 4 * CH), BF),
            pltpu.VMEM((12, 384, 128), F32),
            pltpu.VMEM((3, 3, 64, 128), F32),
            pltpu.VMEM((LF, 10, 3, 48, 128), F32),
            pltpu.VMEM((LF, 10 * COLS, 3 * CH), BF),
            pltpu.VMEM((2, 9 * CH, CH), BF),
            pltpu.VMEM((LF, OUT_ROWS, COLS, CH), BF),
            dma,
            dma,
            dma,
            dma,
            dma((PEERS,)),
            dma((GROUPS,)),
            dma((GROUPS,)),
            dma((NB,)),
            dma,
            dma((PEERS,)),
            dma,
            dma,
            dma((PEERS,)),
            dma((GROUPS,)),
            dma((GROUPS,)),
            dma((PEERS,)),
            dma,
            dma,
            dma,
        ],
        compiler_params=pltpu.CompilerParams(
            collective_id=0, has_side_effects=True, vmem_limit_bytes=60 << 20
        ),
        name="attend_and_decode",
    )(
        tile_rows,
        queries,
        key_tokens,
        value_tokens,
        latent,
        conv_in_weight,
        conv_in_bias,
        norm_gain,
        conv_mid_weight.reshape(3, 9 * CH, CH),
        conv_mid_bias,
    )


def solution(mesh):
    in_specs = (P("seq", None),) * 4 + (P(),) * 6
    out_specs = (P("seq", "sect"), P(None, "seq", "sect", None))
    return jax.shard_map(
        on_device, mesh=mesh, in_specs=in_specs, out_specs=out_specs, check_vma=False
    )
```

profile of v0, /device:TPU:1, one launch (start us, length us, event | category | flops | bytes accessed | tf_op | source)
XLA Modules:
  0.0 71.6 jit_solution(13963647705131587978)
XLA Ops:
  0.6 67.2 %attend_and_decode.1 = (bf16[64,4096]{1,0:T(8,128)(2,1)}, bf16[2,8,40,384]{3,2,1,0:T(8,128)(2,1)}) custom-call(s32[64]{0:T(128)} %tile_rows.1, bf16[64,8192]{1,0:T(8,128)(2,1)} %q.1, bf16[64,8192]{1,0:T(8,128)(2,1)} %k.1, bf16[64,8192]{1,0:T(8,128)(2,1)} %v.1, bf16[4,2560]{1,0:T(4,128)(2,1)} %latent.1, bf16[3,3,3,16,384]{4,3,2,1,0:T(8,128)(2,1)} %w_in.1, ...), custom_call_target="tpu_custom_call" | custom-call | tf_op jit(solution)/shard_map/attend_and_decode/pallas_call | solution.py:448
  67.8 1.9 %copy.14 = bf16[64,4096]{1,0:T(8,128)(2,1)} copy(bf16[64,4096]{1,0:T(8,128)(2,1)} %get-tuple-element.4) | data formatting | bytes 1048576
  69.7 1.9 %copy.15 = bf16[2,8,40,384]{3,2,1,0:T(8,128)(2,1)} copy(bf16[2,8,40,384]{3,2,1,0:T(8,128)(2,1)} %get-tuple-element.5) | data formatting | bytes 983040
where the time goes:
time: 71.9 us; the launch traced here: 71.6 us
  Pallas kernels  67.2 us (93%)
  local copies, waits for them, and re-layouts  3.73 us (5%)
    pallas_call x1, Pallas kernels, on_device(): pl.pallas_call(body, out_shape=(jax.ShapeDtypeStruct((ROWS, PEERS * DH),...  67.2 us
    unnamed x2, local copies, waits for them, and re-layouts  3.73 us

commit v1 on v0

--- a/solution.py
+++ b/solution.py
@@ -89,9 +89,18 @@
     x = (chip // 2) % 4
     z = chip // 8
 
-    def peer(t, sign=1):
-        dz, dx, dy = t // 8, (t // 2) % 4, t % 2
-        return (((z + sign * dz + 4) % 4) * 4 + (x + sign * dx + 4) % 4) * 2 + (y + dy) % 2
+    def around(at):
+        return jnp.where(at >= 4, at - 4, jnp.where(at < 0, at + 4, at))
+
+    steps_x = {1: [around(x + d) for d in range(4)], -1: [around(x - d) for d in range(4)]}
+    steps_y = [y, 1 - y]
+
+    def each_peer(visit, sign=1):
+        @pl.loop(0, 4)
+        def _(dz):
+            peer_z = around(z + sign * dz)
+            for rest in range(GROUP):
+                visit(dz, rest, peer_z, steps_x[sign][rest // 2] * 2 + steps_y[rest % 2])
 
     def device(other_chip, other_core):
         return (sect, other_chip * 2 + other_core)
@@ -106,9 +115,20 @@
     barrier = pltpu.get_barrier_semaphore()
     pl.semaphore_signal(barrier, inc=1, device_id=sibling, device_id_type=MESH)
 
-    @pl.loop(1, PEERS)
-    def _(t):
-        pl.semaphore_signal(barrier, inc=1, device_id=device(peer(t), core), device_id_type=MESH)
+    def others(act, sign=1):
+        def visit(dz, rest, peer_z, low):
+            run = functools.partial(act, dz * GROUP + rest, peer_z * 8 + low)
+            if rest:
+                run()
+            else:
+                pl.when(dz > 0)(run)
+
+        each_peer(visit, sign)
+
+    def greet(t, other):
+        pl.semaphore_signal(barrier, inc=1, device_id=device(other, core), device_id_type=MESH)
+
+    others(greet)
 
     pl.semaphore_wait(barrier, PEERS)
 
@@ -124,7 +144,7 @@
     def lat_needed(holder, tile_chip):
         low = jnp.maximum(2 * tile_chip, 8 * tile_chip - 128) - 1
         high = jnp.minimum(8 * tile_chip + 4, 65 + 2 * tile_chip) + 4
-        first = 8 * (holder % 16)
+        first = 8 * (holder - jnp.where(holder >= 16, 16, 0))
         return (first + 7 >= low) & (first <= high)
 
     lat_cols = pl.ds(pl.multiple_of(1024 * sect, 128), LATW)
@@ -133,10 +153,7 @@
     def _():
         pltpu.make_async_copy(latent.at[:, lat_cols], latbuf.at[core * PEERS], r_l.at[0]).start()
 
-    @pl.loop(1, PEERS)
-    def _(t):
-        other = peer(t)
-
+    def send_latent(t, other):
         @pl.when(lat_needed(chip, other))
         def _():
             remote(
@@ -147,27 +164,19 @@
                 device(other, core),
             ).start()
 
+    others(send_latent)
     mine = head_columns(chip)
     pltpu.make_async_copy(k.at[:, mine], kbuf.at[core_slot(0)], r_k.at[0]).start()
     pltpu.make_async_copy(v.at[:, mine], vbuf.at[core_slot(0)], r_v.at[0]).start()
 
-    @pl.loop(1, PEERS)
-    def _(t):
-        other = peer(t)
+    def send_keys(t, other):
         target = device(other, core)
         cols = head_columns(other)
         group = t // GROUP
         remote(k.at[:, cols], kbuf.at[core_slot(t)], s_k, r_k.at[group], target).start()
         remote(v.at[:, cols], vbuf.at[core_slot(t)], s_v, r_v.at[group], target).start()
 
-    pltpu.make_async_copy(q.at[:, mine], qbuf.at[slot(0)], r_q.at[0]).start()
-
-    @pl.loop(1, PEERS)
-    def _(t):
-        other = peer(t)
-        remote(
-            q.at[:, head_columns(other)], qbuf.at[slot(t)], s_q, r_q.at[t // 4], device(other, core)
-        ).start()
+    others(send_keys)
 
     for a in range(1, 3):
         pltpu.make_async_copy(w_mid.at[a], wm.at[a - 1], w_sem).start()
@@ -197,20 +206,24 @@
     first_row = lax.fori_loop(0, 64, count, jnp.int32(0))
     filled = tile_rows[me]
 
-    @pl.loop(0, PEERS)
-    def _(t):
-        @pl.when(lat_needed(peer(t, -1), chip))
+    def pass_latent(dz, rest, peer_z, low):
+        @pl.when(lat_needed(peer_z * 8 + low, chip))
         def _():
+            t = dz * GROUP + rest
             here = latbuf.at[core * PEERS + t]
             remote(here, here, fs_l.at[t], r_l.at[t], sibling).wait_recv()
             remote(here, here, fs_l.at[t], fr_l.at[t], sibling).start()
 
-    @pl.loop(0, PEERS)
-    def _(t):
-        @pl.when(lat_needed(peer(t, -1), chip))
+    each_peer(pass_latent, -1)
+
+    def await_latent(dz, rest, peer_z, low):
+        @pl.when(lat_needed(peer_z * 8 + low, chip))
         def _():
+            t = dz * GROUP + rest
             there = latbuf.at[(1 - core) * PEERS + t]
             remote(there, there, fs_l.at[t], fr_l.at[t], sibling).wait_recv()
+
+    each_peer(await_latent, -1)
 
     def group_rows(which, g):
         return pl.ds(which * OWN + g * GROUP * ROWS, GROUP * ROWS)
@@ -268,6 +281,16 @@
             ybuf[n * 3 + part] = conv[:, part * 128 : (part + 1) * 128]
 
     hand_on(0)
+
+    def send_queries():
+        pltpu.make_async_copy(q.at[:, mine], qbuf.at[slot(0)], r_q.at[0]).start()
+
+        def send(t, other):
+            remote(
+                q.at[:, head_columns(other)], qbuf.at[slot(t)], s_q, r_q.at[t // 4], device(other, core)
+            ).start()
+
+        others(send)
 
     bias_in = b_in[...].reshape(1, CH)
     gain_row = gain[...].reshape(1, CH)
@@ -323,6 +346,10 @@
             value = total[ro * COLS : (ro + 1) * COLS, :] + bias_mid + centre
             fbuf[f, ro] = jnp.where(ro < 2 * filled, value, 0.0).astype(BF)
         hand_on(2 + f)
+
+        if f == 0:
+            send_queries()
+
     pltpu.make_async_copy(fbuf, frames, out_sem).start()
 
     for which in range(2):
@@ -354,8 +381,7 @@
         top = jnp.max(best, axis=0, keepdims=True) * EXP2_SCALE
         mbuf[which] = jnp.broadcast_to(top, (8, BQ))
 
-    def step(j, with_next):
-        which = j % 2
+    def step(j, which, with_next):
         total = jnp.zeros((DH + 8, BQ), F32)
         if with_next:
             await_queries(j + 1)
@@ -376,12 +402,15 @@
         for u in range(BQ // ROWS):
             t = j * (BQ // ROWS) + u
 
-            def send():
+            low = steps_x[-1][2 * which + u // 2] * 2 + steps_y[u % 2]
+            other = around(z - (j - which) // 2) * 8 + low
+
+            def send(t=t, other=other):
                 remote(
-                    obuf.at[slot(t)], attended.at[:, out_cols], s_o, r_o, device(peer(t, -1), core)
+                    obuf.at[slot(t)], attended.at[:, out_cols], s_o, r_o, device(other, core)
                 ).start()
 
-            if u > 0:
+            if u > 0 or which:
                 send()
             else:
                 pl.when(t > 0)(send)
@@ -398,11 +427,13 @@
         best = score_chunk(q_first, 0, c, best)
     keep_best(best, 0)
 
-    @pl.loop(0, NB - 1)
-    def _(j):
-        step(j, True)
-
-    step(jnp.int32(NB - 1), False)
+    @pl.loop(0, NB // 2 - 1)
+    def _(h):
+        step(2 * h, 0, True)
+        step(2 * h + 1, 1, True)
+
+    step(jnp.int32(NB - 2), 0, True)
+    step(jnp.int32(NB - 1), 1, False)
 
     own = pl.ds(core * OWN, OWN)
     most = kbuf.at[0 : (PEERS - 1) * ROWS]
@@ -412,21 +443,42 @@
     remote(kbuf.at[own], kbuf.at[own], fs_k, r_o, sibling).wait_send()
     remote(kbuf.at[own], kbuf.at[own], fs_v, r_o, sibling).wait_send()
 
-    @pl.loop(0, PEERS)
-    def _(t):
-        @pl.when(lat_needed(peer(t, -1), chip))
+    def end_passed(dz, rest, peer_z, low):
+        @pl.when(lat_needed(peer_z * 8 + low, chip))
         def _():
-            here = latbuf.at[core * PEERS + t]
-            remote(here, here, fs_l.at[t], r_o, sibling).wait_send()
-
-        @pl.when((t > 0) & lat_needed(chip, peer(t)))
+            here = latbuf.at[core * PEERS + dz * GROUP + rest]
+            remote(here, here, fs_l.at[dz * GROUP + rest], r_o, sibling).wait_send()
+
+    each_peer(end_passed, -1)
+
+    def end_latent(t, other):
+        @pl.when(lat_needed(chip, other))
         def _():
             here = latbuf.at[core * PEERS + t]
             remote(here, here, s_l.at[t], r_o, sibling).wait_send()
 
+    others(end_latent)
+
     pltpu.make_async_copy(fbuf, frames, out_sem).wait()
     remote(most, most, s_o, r_o, sibling).wait_send()
     remote(attended, attended, s_o, r_o, sibling).wait_recv()
+
+
+def settle(attended_in, frames_in, attended, frames, abuf, fbuf, sems):
+    pieces = [(attended_in, abuf, attended, 32 * n, 32) for n in range(2)]
+    pieces += [(frames_in, fbuf, frames, n, 1) for n in range(LF)]
+    loads, stores = [], []
+    for n, (source, staged, target, first, count) in enumerate(pieces):
+        part = slice(first, first + count)
+        loads.append(pltpu.make_async_copy(source.at[part], staged.at[part], sems.at[0, n]))
+        stores.append(pltpu.make_async_copy(staged.at[part], target.at[part], sems.at[1, n]))
+    for load in loads:
+        load.start()
+    for load, store in zip(loads, stores):
+        load.wait()
+        store.start()
+    for store in stores:
+        store.wait()
 
 
 def on_device(
@@ -445,7 +497,7 @@
     anywhere = pl.BlockSpec(memory_space=pl.ANY)
     vmem = pl.BlockSpec(memory_space=pltpu.VMEM)
     smem = pl.BlockSpec(memory_space=pltpu.SMEM)
-    return pl.pallas_call(
+    attended, frames = pl.pallas_call(
         body,
         out_shape=(
             jax.ShapeDtypeStruct((ROWS, PEERS * DH), BF),
@@ -507,6 +559,22 @@
         conv_mid_weight.reshape(3, 9 * CH, CH),
         conv_mid_bias,
     )
+    return pl.pallas_call(
+        settle,
+        out_shape=(
+            jax.ShapeDtypeStruct(attended.shape, BF),
+            jax.ShapeDtypeStruct(frames.shape, BF),
+        ),
+        in_specs=[anywhere, anywhere],
+        out_specs=(anywhere, anywhere),
+        scratch_shapes=[
+            pltpu.VMEM(attended.shape, BF),
+            pltpu.VMEM(frames.shape, BF),
+            dma((2, 4)),
+        ],
+        compiler_params=pltpu.CompilerParams(vmem_limit_bytes=60 << 20),
+        name="settle",
+    )(attended, frames)
 
 
 def solution(mesh):

time: 71.9 us -> 53.9 us (0.75)
  Pallas kernels: 67.2 us -> 53.1 us
  local copies, waits for them, and re-layouts: 3.73 us -> 0 us
    pallas_call x1, Pallas kernels: 67.2 us -> 51.1 us  [on_device(): pl.pallas_call(body, out_shape=(jax.ShapeDtypeStruct((ROWS, PEERS * DH),...]
    unnamed x2 -> x0, local copies, waits for them, and re-layouts: 3.73 us -> none
    pallas_call x0 -> x1, Pallas kernels: none -> 1.97 us  [on_device(): pl.pallas_call(settle, out_shape=(jax.ShapeDtypeStruct(attended.shape, BF...]
where the time goes in v1:
time: 53.9 us; the launch traced here: 53.7 us
  Pallas kernels  53.1 us (99%)
  between operations  0.64 us (1%)
    pallas_call x1, Pallas kernels, on_device(): pl.pallas_call(body, out_shape=(jax.ShapeDtypeStruct((ROWS, PEERS * DH),...  51.1 us
    pallas_call x1, Pallas kernels, on_device(): pl.pallas_call(settle, out_shape=(jax.ShapeDtypeStruct(attended.shape, BF...  1.97 us

profile of v1, /device:TPU:1, one launch (start us, length us, event | category | flops | bytes accessed | tf_op | source)
XLA Modules:
  0.0 53.7 jit_solution(5503118707944815323)
XLA Ops:
  0.6 51.1 %attend_and_decode.1 = (bf16[64,4096]{1,0:T(8,128)(2,1)}, bf16[2,8,40,384]{3,2,1,0:T(8,128)(2,1)}) custom-call(s32[64]{0:T(128)} %tile_rows.1, bf16[64,8192]{1,0:T(8,128)(2,1)} %q.1, bf16[64,8192]{1,0:T(8,128)(2,1)} %k.1, bf16[64,8192]{1,0:T(8,128)(2,1)} %v.1, bf16[4,2560]{1,0:T(4,128)(2,1)} %latent.1, bf16[3,3,3,16,384]{4,3,2,1,0:T(8,128)(2,1)} %w_in.1, ...), custom_call_target="tpu_custom_call" | custom-call | tf_op jit(solution)/shard_map/attend_and_decode/pallas_call | solution.py:500
  51.8 2.0 %settle.1 = (bf16[64,4096]{1,0:T(8,128)(2,1)}, bf16[2,8,40,384]{3,2,1,0:T(8,128)(2,1)}) custom-call(bf16[64,4096]{1,0:T(8,128)(2,1)} %get-tuple-element.4.attended_in, bf16[2,8,40,384]{3,2,1,0:T(8,128)(2,1)} %get-tuple-element.5.frames_in), custom_call_target="tpu_custom_call" | custom-call | tf_op jit(solution)/shard_map/settle/pallas_call | solution.py:562

commit v2 on v1

--- a/solution.py
+++ b/solution.py
@@ -92,15 +92,20 @@
     def around(at):
         return jnp.where(at >= 4, at - 4, jnp.where(at < 0, at + 4, at))
 
-    steps_x = {1: [around(x + d) for d in range(4)], -1: [around(x - d) for d in range(4)]}
+    steps_z = {1: [around(z + d) for d in range(4)], -1: [around(z - d) for d in range(4)]}
     steps_y = [y, 1 - y]
 
+    def spread(j, u, sign):
+        late = j >= 4
+        dx = around(jnp.where(late, j - 4, j) + u)
+        peer_y = jnp.where(late, steps_y[1 - u % 2], steps_y[u % 2])
+        return steps_z[sign][u] * 8 + around(x + sign * dx) * 2 + peer_y
+
     def each_peer(visit, sign=1):
-        @pl.loop(0, 4)
-        def _(dz):
-            peer_z = around(z + sign * dz)
-            for rest in range(GROUP):
-                visit(dz, rest, peer_z, steps_x[sign][rest // 2] * 2 + steps_y[rest % 2])
+        @pl.loop(0, NB)
+        def _(j):
+            for u in range(4):
+                visit(j, u, spread(j, u, sign))
 
     def device(other_chip, other_core):
         return (sect, other_chip * 2 + other_core)
@@ -116,12 +121,12 @@
     pl.semaphore_signal(barrier, inc=1, device_id=sibling, device_id_type=MESH)
 
     def others(act, sign=1):
-        def visit(dz, rest, peer_z, low):
-            run = functools.partial(act, dz * GROUP + rest, peer_z * 8 + low)
-            if rest:
+        def visit(j, u, other):
+            run = functools.partial(act, j * 4 + u, other)
+            if u:
                 run()
             else:
-                pl.when(dz > 0)(run)
+                pl.when(j > 0)(run)
 
         each_peer(visit, sign)
 
@@ -206,20 +211,20 @@
     first_row = lax.fori_loop(0, 64, count, jnp.int32(0))
     filled = tile_rows[me]
 
-    def pass_latent(dz, rest, peer_z, low):
-        @pl.when(lat_needed(peer_z * 8 + low, chip))
+    def pass_latent(j, u, other):
+        @pl.when(lat_needed(other, chip))
         def _():
-            t = dz * GROUP + rest
+            t = j * 4 + u
             here = latbuf.at[core * PEERS + t]
             remote(here, here, fs_l.at[t], r_l.at[t], sibling).wait_recv()
             remote(here, here, fs_l.at[t], fr_l.at[t], sibling).start()
 
     each_peer(pass_latent, -1)
 
-    def await_latent(dz, rest, peer_z, low):
-        @pl.when(lat_needed(peer_z * 8 + low, chip))
+    def await_latent(j, u, other):
+        @pl.when(lat_needed(other, chip))
         def _():
-            t = dz * GROUP + rest
+            t = j * 4 + u
             there = latbuf.at[(1 - core) * PEERS + t]
             remote(there, there, fs_l.at[t], fr_l.at[t], sibling).wait_recv()
 
@@ -246,7 +251,8 @@
             dz = (z - other // 8 + 4) % 4
             dx = (x - (other // 2) % 4 + 4) % 4
             dy = (y - other % 2 + 2) % 2
-            rows4 = latbuf[(holder % 2) * PEERS + dz * 8 + dx * 2 + dy].astype(F32)
+            turn = (dx - dz + 4) % 4 + 4 * ((dz + dy) % 2)
+            rows4 = latbuf[(holder % 2) * PEERS + turn * 4 + dz].astype(F32)
             wanted = jnp.where(inside, safe % 4, -1)
             row = jnp.sum(jnp.where(sub_iota == wanted, rows4, 0.0), axis=0, keepdims=True)
             picked[f * 8 + r : f * 8 + r + 1, :] = row
@@ -402,8 +408,7 @@
         for u in range(BQ // ROWS):
             t = j * (BQ // ROWS) + u
 
-            low = steps_x[-1][2 * which + u // 2] * 2 + steps_y[u % 2]
-            other = around(z - (j - which) // 2) * 8 + low
+            other = spread(j, u, -1)
 
             def send(t=t, other=other):
                 remote(
@@ -443,11 +448,11 @@
     remote(kbuf.at[own], kbuf.at[own], fs_k, r_o, sibling).wait_send()
     remote(kbuf.at[own], kbuf.at[own], fs_v, r_o, sibling).wait_send()
 
-    def end_passed(dz, rest, peer_z, low):
-        @pl.when(lat_needed(peer_z * 8 + low, chip))
+    def end_passed(j, u, other):
+        @pl.when(lat_needed(other, chip))
         def _():
-            here = latbuf.at[core * PEERS + dz * GROUP + rest]
-            remote(here, here, fs_l.at[dz * GROUP + rest], r_o, sibling).wait_send()
+            here = latbuf.at[core * PEERS + j * 4 + u]
+            remote(here, here, fs_l.at[j * 4 + u], r_o, sibling).wait_send()
 
     each_peer(end_passed, -1)
 

time: 53.9 us -> 52.5 us (0.974)
  the two profiles are of different devices: /device:TPU:1 before, /device:TPU:8 now
where the time goes in v2:
time: 52.5 us; the launch traced here: 52.3 us
  Pallas kernels  51.7 us (98%)
  between operations  0.64 us (1%)
    pallas_call x1, Pallas kernels, on_device(): pl.pallas_call(body, out_shape=(jax.ShapeDtypeStruct((ROWS, PEERS * DH),...  49.7 us
    pallas_call x1, Pallas kernels, on_device(): pl.pallas_call(settle, out_shape=(jax.ShapeDtypeStruct(attended.shape, BF...  1.97 us

profile of v2, /device:TPU:8, one launch (start us, length us, event | category | flops | bytes accessed | tf_op | source)
XLA Modules:
  0.0 52.3 jit_solution(16134398219274633478)
XLA Ops:
  0.6 49.7 %attend_and_decode.1 = (bf16[64,4096]{1,0:T(8,128)(2,1)}, bf16[2,8,40,384]{3,2,1,0:T(8,128)(2,1)}) custom-call(s32[64]{0:T(128)} %tile_rows.1, bf16[64,8192]{1,0:T(8,128)(2,1)} %q.1, bf16[64,8192]{1,0:T(8,128)(2,1)} %k.1, bf16[64,8192]{1,0:T(8,128)(2,1)} %v.1, bf16[4,2560]{1,0:T(4,128)(2,1)} %latent.1, bf16[3,3,3,16,384]{4,3,2,1,0:T(8,128)(2,1)} %w_in.1, ...), custom_call_target="tpu_custom_call" | custom-call | tf_op jit(solution)/shard_map/attend_and_decode/pallas_call | solution.py:505
  50.3 2.0 %settle.1 = (bf16[64,4096]{1,0:T(8,128)(2,1)}, bf16[2,8,40,384]{3,2,1,0:T(8,128)(2,1)}) custom-call(bf16[64,4096]{1,0:T(8,128)(2,1)} %get-tuple-element.4.attended_in, bf16[2,8,40,384]{3,2,1,0:T(8,128)(2,1)} %get-tuple-element.5.frames_in), custom_call_target="tpu_custom_call" | custom-call | tf_op jit(solution)/shard_map/settle/pallas_call | solution.py:567

commit v3 on v2

--- a/solution.py
+++ b/solution.py
@@ -358,16 +358,9 @@
 
     pltpu.make_async_copy(fbuf, frames, out_sem).start()
 
-    for which in range(2):
-        for g in range(GROUPS):
-            rows = slice(which * OWN + g * GROUP * ROWS, which * OWN + (g + 1) * GROUP * ROWS)
-
-            @pl.when(core != which)
-            def _():
-                remote(kbuf.at[rows], kbuf.at[rows], fs_k, fr_k.at[g], sibling).wait_recv()
-                remote(vbuf.at[rows], vbuf.at[rows], fs_v, fr_v.at[g], sibling).wait_recv()
-
-            vt[0:DH, rows] = vbuf[rows, :].T
+    for g in range(GROUPS):
+        rows = group_rows(1 - core, g)
+        remote(kbuf.at[rows], kbuf.at[rows], fs_k, fr_k.at[g], sibling).wait_recv()
 
     def block(j):
         return pl.ds(pl.multiple_of(j * BQ, BQ), BQ)
@@ -431,6 +424,16 @@
     for c in range(KEYS // BK):
         best = score_chunk(q_first, 0, c, best)
     keep_best(best, 0)
+
+    for which in range(2):
+        for g in range(GROUPS):
+            rows = slice(which * OWN + g * GROUP * ROWS, which * OWN + (g + 1) * GROUP * ROWS)
+
+            @pl.when(core != which)
+            def _():
+                remote(vbuf.at[rows], vbuf.at[rows], fs_v, fr_v.at[g], sibling).wait_recv()
+
+            vt[0:DH, rows] = vbuf[rows, :].T
 
     @pl.loop(0, NB // 2 - 1)
     def _(h):

time: 52.5 us -> 52.9 us (level)
  the two profiles are of different devices: /device:TPU:8 before, /device:TPU:1 now
where the time goes in v3:
time: 52.9 us; the launch traced here: 51.8 us
  Pallas kernels  51.2 us (97%)
  between operations  0.64 us (1%)
    pallas_call x1, Pallas kernels, on_device(): pl.pallas_call(body, out_shape=(jax.ShapeDtypeStruct((ROWS, PEERS * DH),...  49.2 us
    pallas_call x1, Pallas kernels, on_device(): pl.pallas_call(settle, out_shape=(jax.ShapeDtypeStruct(attended.shape, BF...  1.97 us

profile of v3, /device:TPU:1, one launch (start us, length us, event | category | flops | bytes accessed | tf_op | source)
XLA Modules:
  0.0 51.8 jit_solution(5229402333042912618)
XLA Ops:
  0.6 49.2 %attend_and_decode.1 = (bf16[64,4096]{1,0:T(8,128)(2,1)}, bf16[2,8,40,384]{3,2,1,0:T(8,128)(2,1)}) custom-call(s32[64]{0:T(128)} %tile_rows.1, bf16[64,8192]{1,0:T(8,128)(2,1)} %q.1, bf16[64,8192]{1,0:T(8,128)(2,1)} %k.1, bf16[64,8192]{1,0:T(8,128)(2,1)} %v.1, bf16[4,2560]{1,0:T(4,128)(2,1)} %latent.1, bf16[3,3,3,16,384]{4,3,2,1,0:T(8,128)(2,1)} %w_in.1, ...), custom_call_target="tpu_custom_call" | custom-call | tf_op jit(solution)/shard_map/attend_and_decode/pallas_call | solution.py:508
  49.9 2.0 %settle.1 = (bf16[64,4096]{1,0:T(8,128)(2,1)}, bf16[2,8,40,384]{3,2,1,0:T(8,128)(2,1)}) custom-call(bf16[64,4096]{1,0:T(8,128)(2,1)} %get-tuple-element.4.attended_in, bf16[2,8,40,384]{3,2,1,0:T(8,128)(2,1)} %get-tuple-element.5.frames_in), custom_call_target="tpu_custom_call" | custom-call | tf_op jit(solution)/shard_map/settle/pallas_call | solution.py:570
